TPU v7x, 256 devices: a whole 4x4x8 slice. The times are simulated.
256 devices in a mesh: tensor: 4 (over x), shard: 64 (over z, y, core).
Axes of the slice: x: 4, y: 4, z: 8, core: 2. Of those that a mesh axis runs over, the one named last changes fastest.
Arguments:
- proj_grads: bfloat16 [128, 2, 1152, 1024], P('shard', None, None, 'tensor'), may hold values from -60 to 60
- kv_grads: bfloat16 [512, 1152, 512], P(('tensor', 'shard')), may hold values from -60 to 60
- gain_grads: bfloat16 [512, 2, 256], P(('tensor', 'shard')), may hold values from -60 to 60
- proj_master: float32 [2, 1152, 1024], P(None, 'shard', 'tensor'), may hold values from -0.3125 to 0.3125
- proj_m: float32 [2, 1152, 1024], P(None, 'shard', 'tensor'), may hold values from -1.5 to 1.5
- proj_v: float32 [2, 1152, 1024], P(None, 'shard', 'tensor'), may hold values from 0.02 to 0.5
- kv_master: float32 [1152, 512], P('shard', 'tensor'), may hold values from -0.3125 to 0.3125
- kv_m: float32 [1152, 512], P('shard', 'tensor'), may hold values from -1.5 to 1.5
- kv_v: float32 [1152, 512], P('shard', 'tensor'), may hold values from 0.02 to 0.5
- gains: float32 [2, 256], replicated, may hold values from 0.1 to 1.9
- gains_m: float32 [2, 256], replicated, may hold values from -6 to 6
- gains_v: float32 [2, 256], replicated, may hold values from 0.25 to 4
Outputs:
- proj_master_new: float32 [2, 1152, 1024], P(None, 'shard', 'tensor')
- proj_m_new: float32 [2, 1152, 1024], P(None, 'shard', 'tensor')
- proj_v_new: float32 [2, 1152, 1024], P(None, 'shard', 'tensor')
- proj_weights: bfloat16 [2, 1152, 1024], P(None, None, 'tensor')
- kv_master_new: float32 [1152, 512], P('shard', 'tensor')
- kv_m_new: float32 [1152, 512], P('shard', 'tensor')
- kv_v_new: float32 [1152, 512], P('shard', 'tensor')
- kv_weights: bfloat16 [1152, 512], replicated
- gains_new: float32 [2, 256], replicated
- gains_m_new: float32 [2, 256], replicated
- gains_v_new: float32 [2, 256], replicated
All inputs are finite; a program needn't handle non-finite values.
Results may differ from a plain program's by a relative error of at most 0.0004.
Values may be sent and summed in bfloat16 or wider, within the bound.
A program may use at most 64 MiB of HBM per device.

v0:
```python
import math

import jax
import jax.numpy as jnp
from jax import lax
from jax.sharding import PartitionSpec as P

PARAMS = 2949632


beta_one = 0.9
beta_two = 0.95
learn_rate = 0.01
decay_rate = 0.1
epsilon = 1e-08
step_count = 10


def adamw_step(master, moment, second, update_grad, decay):
    moment_new = beta_one * moment + (1.0 - beta_one) * update_grad
    second_new = beta_two * second + (1.0 - beta_two) * update_grad * update_grad
    first_hat = moment_new / (1.0 - beta_one**step_count)
    second_hat = second_new / (1.0 - beta_two**step_count)
    master_new = master - learn_rate * (
        first_hat / (jnp.sqrt(second_hat) + epsilon) + decay * master
    )
    return (master_new, moment_new, second_new)


def shards(
    proj_grads,
    kv_grads,
    gain_grads,
    proj_master,
    proj_m,
    proj_v,
    kv_master,
    kv_m,
    kv_v,
    gains,
    gains_m,
    gains_v,
):
    proj_local = jnp.sum(proj_grads, axis=0, dtype=jnp.float32)
    kv_local = jnp.sum(kv_grads, axis=0, dtype=jnp.float32)
    gain_local = jnp.sum(gain_grads, axis=0, dtype=jnp.float32)
    gain_sum = lax.psum(gain_local, ("tensor", "shard"))
    proj_owned, kv_row_part = (
        lax.psum_scatter(proj_local, "shard", scatter_dimension=1, tiled=True),
        lax.psum_scatter(kv_local, "shard", scatter_dimension=0, tiled=True),
    )
    kv_owned = lax.psum_scatter(kv_row_part, "tensor", scatter_dimension=1, tiled=True)
    owned_square = jnp.sum(proj_owned * proj_owned) + jnp.sum(kv_owned * kv_owned)
    norm_square = lax.psum(owned_square, ("tensor", "shard")) + jnp.sum(gain_sum * gain_sum)
    clip_factor = jnp.minimum(1.0, math.sqrt(PARAMS) / jnp.sqrt(norm_square))
    proj_new, proj_m_new, proj_v_new = adamw_step(
        proj_master, proj_m, proj_v, clip_factor * proj_owned, decay_rate
    )
    kv_new, kv_m_new, kv_v_new = adamw_step(
        kv_master, kv_m, kv_v, clip_factor * kv_owned, decay_rate
    )
    gains_new, gains_m_new, gains_v_new = adamw_step(
        gains, gains_m, gains_v, clip_factor * gain_sum, 0.0
    )
    proj_half = proj_new.astype(jnp.bfloat16)
    kv_half = kv_new.astype(jnp.bfloat16)
    kv_wide = lax.all_gather(kv_half, "tensor", axis=1, tiled=True)
    proj_weights, kv_weights = (
        lax.all_gather(proj_half, "shard", axis=1, tiled=True),
        lax.all_gather(kv_wide, "shard", axis=0, tiled=True),
    )
    return (
        proj_new,
        proj_m_new,
        proj_v_new,
        proj_weights,
        kv_new,
        kv_m_new,
        kv_v_new,
        kv_weights,
        gains_new,
        gains_m_new,
        gains_v_new,
    )


def solution(mesh):
    placed = (
        P("shard", None, None, "tensor"),
        P(("tensor", "shard"), None, None),
        P(("tensor", "shard"), None, None),
        P(None, "shard", "tensor"),
        P(None, "shard", "tensor"),
        P(None, "shard", "tensor"),
        P("shard", "tensor"),
        P("shard", "tensor"),
        P("shard", "tensor"),
        P(),
        P(),
        P(),
    )
    return jax.shard_map(
        shards,
        mesh=mesh,
        in_specs=placed,
        out_specs=(
            P(None, "shard", "tensor"),
            P(None, "shard", "tensor"),
            P(None, "shard", "tensor"),
            P(None, None, "tensor"),
            P("shard", "tensor"),
            P("shard", "tensor"),
            P("shard", "tensor"),
            P(),
            P(),
            P(),
            P(),
        ),
        check_vma=False,
    )
```

profile of v0, /device:TPU:1, one launch (start us, length us, event | category | flops | bytes accessed | tf_op | source)
XLA Modules:
  0.0 487.7 jit_solution(7765557723649341525)
XLA Ops:
  7.2 0.0 all-reduce.6.cloned.1.call-start
  7.2 2.3 convert_reduce_fusion.1
  9.5 7.6 %copy.25 = f32[2,1152,256]{2,0,1:T(2,128)} copy(f32[2,1152,256]{2,1,0:T(8,128)S(1)} %convert_reduce_fusion.1) | data formatting | bytes 4718592 | tf_op jit(solution)/shard_map/reduce_sum | solution.py:44
  17.2 2.0 convert_reduce_fusion
  19.3 0.0 reduce-scatter.2.cloned.1.call-start
  19.3 0.5 copy-done.11
  19.9 0.6 dynamic-slice
  21.1 197.5 %all-reduce.6.cloned.1.call-done = (f32[2,1152,256]{2,0,1:T(2,128)}, f32[1152,512]{1,0:T(8,128)}) async-done(((f32[2,1152,256]{2,0,1:T(2,128)}, f32[1152,512]{1,0:T(8,128)}), (f32[2,1152,256]{2,0,1:T(2,128)}, f32[1152,512]{1,0:T(8,128)})) %all-reduce.6.cloned.1.call-update) | async-done | bytes 4718608
  218.6 1.5 constant_dynamic-slice_fusion
  220.1 0.0 all-gather.4.cloned.1.call-start
  220.2 1.4 multiply_reduce_fusion
  221.6 21.1 %reduce-scatter.2.cloned.1.call-done = f32[18,128]{1,0:T(8,128)} async-done(((f32[18,512]{1,0:T(8,128)}), f32[18,128]{1,0:T(8,128)}) %reduce-scatter.2.cloned.1.call-update) | async-done | bytes 9232 | tf_op jit(solution)/shard_map/reduce_scatter | solution.py:52
  242.7 1.3 multiply_reduce_fusion.1
  245.3 78.1 %all-reduce.2 = (f32[]{:T(128)}, f32[2,256]{1,0:T(2,128)S(1)}) all-reduce(f32[]{:T(128)S(6)} %add.61, f32[2,256]{1,0:T(2,128)S(1)} %convert_reduce_fusion.2), channel_id=1, replica_groups=mesh['tensor'=4,'shard'=64] {'tensor','shard'}, use_global_device_ids=true, to_apply=%region_7.0 | all-reduce | flops 513 | bytes 4104 | tf_op jit(solution)/shard_map/psum | solution.py:54
  323.5 0.6 multiply_reduce_fusion.2
  325.4 1.5 fusion.6
  327.0 0.0 all-gather.6.cloned.1.call-start
  327.1 1.3 fusion.4
  328.4 8.5 %all_gather.10 = bf16[18,512]{1,0:T(8,128)(2,1)} all-gather(bf16[18,128]{1,0:T(8,128)(2,1)S(1)} %get-tuple-element.29), channel_id=1, replica_groups=mesh['tensor'=4,'shard'=64] {'tensor'}, dimensions={1}, use_global_device_ids=true | all-gather | bytes 23040 | tf_op jit(solution)/shard_map/all_gather | solution.py:67
  336.9 0.6 multiply_subtract_fusion.2
  337.5 63.2 %all-gather.4.cloned.1.call-done = bf16[2,1152,256]{2,0,1:T(2,128)(2,1)} async-done(((bf16[2,18,256]{2,0,1:T(2,128)(2,1)}), bf16[2,1152,256]{2,0,1:T(2,128)(2,1)}) %all-gather.4.cloned.1.call-update) | async-done | bytes 1179664 | tf_op jit(solution)/shard_map/all_gather | solution.py:69
  400.7 2.4 copy.26
  403.2 74.9 %all-gather.6.cloned.1.call-done = bf16[64,18,512]{2,1,0:T(8,128)(2,1)} async-done(((bf16[1,18,512]{2,1,0:T(8,128)(2,1)}), bf16[64,18,512]{2,1,0:T(8,128)(2,1)}) %all-gather.6.cloned.1.call-update) | async-done | bytes 1179664 | tf_op jit(solution)/shard_map/all_gather | solution.py:70
  478.1 3.1 reshape.23
  (28 shorter events, 0.1 us)
Async XLA Ops:
  7.2 211.4 %all-reduce.6.cloned.1.call-start = ((), (), s32[]{:S(2)}) async-start(), calls=%async_computation.4 | async-start | bytes 9437184
  9.5 7.7 %copy-start = (bf16[2,1152,512]{2,1,0:T(8,128)(2,1)S(1)}, bf16[2,1152,512]{2,1,0:T(8,128)(2,1)}, u32[]{:S(2)}) copy-start(bf16[2,1152,512]{2,1,0:T(8,128)(2,1)} %param.13) | copy-start | bytes 7077892
  19.2 0.7 copy-start.11
  19.2 201.0 %copy-start.7 = (bf16[2,2,256]{2,1,0:T(2,128)(2,1)S(1)}, bf16[2,2,256]{2,1,0:T(2,128)(2,1)}, u32[]{:S(2)}) copy-start(bf16[2,2,256]{2,1,0:T(2,128)(2,1)} %param.14) | copy-start | bytes 6148
  19.2 306.2 %copy-start.1 = (f32[2,18,256]{2,0,1:T(2,128)S(1)}, f32[2,18,256]{2,0,1:T(2,128)}, u32[]{:S(2)}) copy-start(f32[2,18,256]{2,0,1:T(2,128)} %param.15) | copy-start | bytes 110596
  19.2 306.2 %copy-start.2 = (f32[2,18,256]{2,0,1:T(2,128)S(1)}, f32[2,18,256]{2,0,1:T(2,128)}, u32[]{:S(2)}) copy-start(f32[2,18,256]{2,0,1:T(2,128)} %param.16) | copy-start | bytes 110596
  19.2 306.2 %copy-start.3 = (f32[2,18,256]{2,0,1:T(2,128)S(1)}, f32[2,18,256]{2,0,1:T(2,128)}, u32[]{:S(2)}) copy-start(f32[2,18,256]{2,0,1:T(2,128)} %param.17) | copy-start | bytes 110596
  19.2 307.9 %copy-start.4 = (f32[18,128]{1,0:T(8,128)S(1)}, f32[18,128]{1,0:T(8,128)}, u32[]{:S(2)}) copy-start(f32[18,128]{1,0:T(8,128)} %param.18) | copy-start | bytes 27652
  19.2 307.9 %copy-start.5 = (f32[18,128]{1,0:T(8,128)S(1)}, f32[18,128]{1,0:T(8,128)}, u32[]{:S(2)}) copy-start(f32[18,128]{1,0:T(8,128)} %param.19) | copy-start | bytes 27652
  19.2 307.9 %copy-start.6 = (f32[18,128]{1,0:T(8,128)S(1)}, f32[18,128]{1,0:T(8,128)}, u32[]{:S(2)}) copy-start(f32[18,128]{1,0:T(8,128)} %param.20) | copy-start | bytes 27652
  19.2 317.7 %copy-start.8 = (f32[2,256]{1,0:T(2,128)S(1)}, f32[2,256]{1,0:T(2,128)}, u32[]{:S(2)}) copy-start(f32[2,256]{1,0:T(2,128)} %param.21) | copy-start | bytes 6148
  19.2 317.7 %copy-start.9 = (f32[2,256]{1,0:T(2,128)S(1)}, f32[2,256]{1,0:T(2,128)}, u32[]{:S(2)}) copy-start(f32[2,256]{1,0:T(2,128)} %param.22) | copy-start | bytes 6148
  19.3 317.7 %copy-start.10 = (f32[2,256]{1,0:T(2,128)S(1)}, f32[2,256]{1,0:T(2,128)}, u32[]{:S(2)}) copy-start(f32[2,256]{1,0:T(2,128)} %param.23) | copy-start | bytes 6148
  19.3 223.4 %reduce-scatter.2.cloned.1.call-start = ((), (), s32[]{:S(2)}) async-start(), calls=%async_computation.1 | async-start | bytes 61440 | tf_op jit(solution)/shard_map/reduce_scatter | solution.py:52
  220.1 180.6 %all-gather.4.cloned.1.call-start = ((), (), s32[]{:S(2)}) async-start(), calls=%async_computation.2 | async-start | bytes 1198080 | tf_op jit(solution)/shard_map/all_gather | solution.py:69
  327.0 151.1 %all-gather.6.cloned.1.call-start = ((), (), s32[]{:S(2)}) async-start(), calls=%async_computation.3 | async-start | bytes 1597440 | tf_op jit(solution)/shard_map/all_gather | solution.py:70
Sparse Core Ops, SparseCore 0:
  19.4 199.1 all-reduce.5
  221.8 20.8 reduce-scatter.1
  327.1 73.5 all-gather.3
  403.4 74.6 all-gather.5
where the time goes:
time: 488 us
  waiting for transfers between devices  357 us (73%)
  blocking collectives  86.6 us (18%)
  between operations  17.2 us (4%)
  local copies, waits for them, and re-layouts  15.8 us (3%)
  other arithmetic  11.1 us (2%)
    unnamed x5, waiting for transfers between devices  198 us
    psum x1, blocking collectives, shards(): lax.psum(owned_square, ('tensor', 'shard')) + jnp.sum(gain_sum * gain_sum)  78.1 us
    all_gather x1, waiting for transfers between devices, shards(): lax.all_gather(kv_wide, 'shard', axis=0, tiled=True)  74.9 us
    all_gather x1, waiting for transfers between devices, shards(): lax.all_gather(proj_half, 'shard', axis=1, tiled=True)  63.2 us
    reduce_scatter x1, waiting for transfers between devices, shards(): lax.psum_scatter(kv_row_part, 'tensor', scatter_dimension=1, tiled=True)  21.1 us
  transfers between devices with their start and end apart: 4, of which 4 were waited for; matrix products, arithmetic and copies ran while one was open for 1% of the time, Pallas kernels for 0%

commit v1 on v0

v1 whole, which is shorter than its diff:
```python
import math

import jax
import jax.numpy as jnp
from jax import lax
from jax.experimental import pallas as pl
from jax.experimental.pallas import tpu as pltpu
from jax.sharding import PartitionSpec as P

PARAMS = 2949632
MESH = pl.DeviceIdType.MESH
F32, BF16 = jnp.float32, jnp.bfloat16

NZ, NY, NC, NX = 8, 4, 2, 4
R = 18
ZR = NY * NC * R
LANES = 128

beta_one = 0.9
beta_two = 0.95
learn_rate = 0.01
decay_rate = 0.1
epsilon = 1e-08
step_count = 10


def adamw_step(master, moment, second, update_grad, decay):
    moment_new = beta_one * moment + (1.0 - beta_one) * update_grad
    second_new = beta_two * second + (1.0 - beta_two) * update_grad * update_grad
    first_hat = moment_new / (1.0 - beta_one**step_count)
    second_hat = second_new / (1.0 - beta_two**step_count)
    master_new = master - learn_rate * (
        first_hat / (jnp.sqrt(second_hat) + epsilon) + decay * master
    )
    return (master_new, moment_new, second_new)


def clip_of(tile):
    row = lax.broadcasted_iota(jnp.int32, tile.shape, 0)
    terms = jnp.where(row < 4, tile * tile, jnp.where(row == 4, tile, 0.0))
    norm_square = jnp.sum(jnp.sum(terms, axis=0, keepdims=True), axis=1, keepdims=True)
    return jnp.minimum(1.0, math.sqrt(PARAMS) / jnp.sqrt(norm_square))


class Links:
    def __init__(self, send_sems, recv_sems, local_sems):
        self.send_sems, self.recv_sems, self.local_sems = send_sems, recv_sems, local_sems
        self.started, self.locals = [], 0

    def send(self, src, dst, device):
        number = len(self.started)
        copy = pltpu.make_async_remote_copy(
            src_ref=src,
            dst_ref=dst,
            send_sem=self.send_sems.at[number],
            recv_sem=self.recv_sems.at[number],
            device_id=device,
            device_id_type=MESH,
        )
        copy.start()
        self.started.append(copy)
        return copy

    def local(self, src, dst):
        copy = pltpu.make_async_copy(src, dst, self.local_sems.at[self.locals])
        self.locals += 1
        copy.start()
        return copy

    def finish(self):
        for copy in self.started:
            copy.wait_send()


N_COPIES = 176


def scatter_ring(links, n, pos, device, view, slot):
    half = n // 2
    copies = {}

    def step(way, part, d):
        dest = lax.rem(pos + way * d + n, n)
        copies[way, part, d] = links.send(view(dest, part), slot(way, part, d), device(lax.rem(pos + way + n, n)))

    def take(way, part, d):
        copies[way, part, d].wait_recv()
        dest = lax.rem(pos + way * (d - 1) + n, n)
        ref, got = view(dest, part), slot(way, part, d)
        ref[...] = ref[...] + got[...]

    for way in (1, -1):
        step(way, 0 if way == 1 else 1, half)
    if half > 1:
        for way in (1, -1):
            step(way, 1 if way == 1 else 0, half - 1)
    for d in range(half - 1, 0, -1):
        yield
        for way in (1, -1):
            lead = 0 if way == 1 else 1
            take(way, lead, d + 1)
            step(way, lead, d)
        if d < half - 1:
            for way in (1, -1):
                other = 1 if way == 1 else 0
                take(way, other, d + 1)
                step(way, other, d)
    yield
    for way in (1, -1):
        for part in (0, 1):
            if (way, part, 1) in copies:
                take(way, part, 1)


def run(*generators):
    waiting = list(generators)
    while waiting:
        waiting = [g for g in waiting if next(g, "end") != "end"]


def step_kernel(
    pg, kg, gg, p_master, p_m, p_v, k_master, k_m, k_v,
    psum_o, ksum_o, tile_o, pw_o, kw_o,
    pgv, kgv, PA, PB, KK, RA, RB, RK, T,
    rAy, rBz, rKx, rAz0, rAz1, rBy, rKy, K3, rKz0, rKz1,
    tc, tx, ty, tz, S72, W96, G, FK, T5,
    send_sems, recv_sems, local_sems,
):
    shard, x = lax.axis_index("shard"), lax.axis_index("tensor")
    c = lax.rem(shard, NC)
    y = lax.rem(shard // NC, NY)
    z = shard // (NC * NY)
    oc = 1 - c

    def device(z=z, y=y, c=c, x=x):
        return {"shard": (z * NY + y) * NC + c, "tensor": x}

    links = Links(send_sems, recv_sems, local_sems)
    sibling = device(c=oc)
    others = [sibling]
    others += [device(x=lax.rem(x + d, NX)) for d in range(1, NX)]
    others += [device(y=lax.rem(y + d, NY)) for d in range(1, NY)]
    others += [device(z=lax.rem(z + d, NZ)) for d in range(1, NZ)]

    k_in = links.local(kg, kgv)
    p_in = links.local(pg, pgv)
    barrier = pltpu.get_barrier_semaphore()
    for other in others:
        pl.semaphore_signal(barrier, inc=1, device_id=other, device_id_type=MESH)

    gain = gg[0].astype(F32) + gg[1].astype(F32)
    tc[c] = jnp.zeros((8, LANES), F32)
    for i in range(2):
        for h in range(2):
            tc[c, 2 * i + h : 2 * i + h + 1, :] = gain[i : i + 1, h * LANES : (h + 1) * LANES]

    k_in.wait()
    barrier_done = False
    k_cores = []
    for dx in (2, 1, 3, 0):
        xx = lax.rem(x + dx, NX)
        col = pl.ds(pl.multiple_of(xx * LANES, LANES), LANES)

        @pl.loop(0, 2)
        def _(zh):
            for zl in range(4):
                rows = pl.ds(pl.multiple_of((zh * 4 + zl) * ZR, 16), ZR)
                T[...] = kgv[0, rows, col].astype(F32) + kgv[1, rows, col].astype(F32)
                for k in range(NY * NC):
                    KK[k % NC, xx, k // NC, zh, R * zl : R * zl + R, :] = T[R * k : R * k + R, :]

        if not barrier_done:
            pl.semaphore_wait(barrier, len(others))
            barrier_done = True
        k_cores.append((xx, links.send(KK.at[oc, xx], RK.at[xx], sibling)))

    p_in.wait()
    for p in range(2):

        @pl.loop(0, NZ)
        def _(zz):
            rows = pl.ds(pl.multiple_of(zz * ZR, 16), ZR)
            for h in range(2):
                col = slice(h * LANES, (h + 1) * LANES)
                T[...] = pgv[0, p, rows, col].astype(F32) + pgv[1, p, rows, col].astype(F32)
                for k in range(NY * NC):
                    yy, cc = k // NC, k % NC
                    q = 2 * p + h
                    if q < 2:
                        PA[cc, yy, zz, R * q : R * q + R, :] = T[R * k : R * k + R, :]
                    elif q == 2:
                        PA[cc, yy, zz, 36:40, :] = T[R * k : R * k + 4, :]
                        PB[cc, zz, yy, 0:14, :] = T[R * k + 4 : R * k + R, :]
                    else:
                        PB[cc, zz, yy, 14:32, :] = T[R * k : R * k + R, :]

    b_core = links.send(PB.at[oc], RB, sibling)
    a_core = links.send(PA.at[oc], RA, sibling)

    for xx, copy in k_cores:
        copy.wait_recv()
        KK[c, xx] = KK[c, xx] + RK[xx]
    ring_kx = scatter_ring(
        links, NX, x, lambda i: device(x=i),
        lambda i, part: KK.at[c, i, 2 * part : 2 * part + 2],
        lambda way, part, d: rKx.at[(1 - way) // 2, part, d - 1],
    )
    next(ring_kx)
    b_core.wait_recv()

    @pl.loop(0, NZ)
    def _(zz):
        PB[c, zz] = PB[c, zz] + RB[zz]

    ring_bz = scatter_ring(
        links, NZ, z, lambda i: device(z=i),
        lambda i, part: PB.at[c, i, 2 * part : 2 * part + 2],
        lambda way, part, d: rBz.at[(1 - way) // 2, part, d - 1],
    )
    next(ring_bz)
    a_core.wait_recv()

    @pl.loop(0, NY)
    def _(yy):
        PA[c, yy] = PA[c, yy] + RA[yy]

    ring_ay = scatter_ring(
        links, NY, y, lambda i: device(y=i),
        lambda i, part: PA.at[c, i, 4 * part : 4 * part + 4],
        lambda way, part, d: rAy.at[(1 - way) // 2, part, d - 1],
    )
    next(ring_ay)

    run(ring_ay, ring_bz, ring_kx)

    cut_a, cut_b = (slice(0, 24), slice(24, 40)), (slice(0, 16), slice(16, 32))
    ring_az = scatter_ring(
        links, NZ, z, lambda i: device(z=i),
        lambda i, part: PA.at[c, y, i, cut_a[part]],
        lambda way, part, d: (rAz0, rAz1)[part].at[(1 - way) // 2, d - 1],
    )
    ring_by = scatter_ring(
        links, NY, y, lambda i: device(y=i),
        lambda i, part: PB.at[c, z, i, cut_b[part]],
        lambda way, part, d: rBy.at[(1 - way) // 2, part, d - 1],
    )
    ring_ky = scatter_ring(
        links, NY, y, lambda i: device(y=i),
        lambda i, part: KK.at[c, x, i, part],
        lambda way, part, d: rKy.at[(1 - way) // 2, part, d - 1],
    )
    run(ring_ky, ring_az, ring_by)

    K3[...] = jnp.zeros_like(K3)
    for zz in range(NZ):
        K3[zz, 0:R, :] = KK[c, x, y, zz // 4, R * (zz % 4) : R * (zz % 4) + R, :]
    cut_k = (slice(0, 16), slice(16, 24))
    ring_kz = scatter_ring(
        links, NZ, z, lambda i: device(z=i),
        lambda i, part: K3.at[i, cut_k[part]],
        lambda way, part, d: (rKz0, rKz1)[part].at[(1 - way) // 2, d - 1],
    )
    run(ring_kz)

    S72[0:40, :] = PA[c, y, z]
    S72[40:72, :] = PB[c, z, y]
    p_sum, k_sum = S72[...], K3[z]
    squares = jnp.sum(p_sum * p_sum, axis=0, keepdims=True) + jnp.sum(k_sum * k_sum, axis=0, keepdims=True)
    tc[c, 4:5, :] = squares
    for slots, n, me, where in (
        (tc, NC, c, lambda i: device(c=i)),
        (tx, NX, x, lambda i: device(x=i)),
        (ty, NY, y, lambda i: device(y=i)),
        (tz, NZ, z, lambda i: device(z=i)),
    ):
        if slots is not tc:
            slots[me] = total
        copies = []
        for d in range(1, n):
            copies.append(links.send(slots.at[me], slots.at[me], where(lax.rem(me + d, n))))
        for copy in copies:
            copy.wait_recv()
        total = slots[0]
        for i in range(1, n):
            total = total + slots[i]
    tile_o[...] = total
    clip = clip_of(total)

    W96[...] = jnp.zeros_like(W96)
    for p in range(2):
        for h in range(2):
            q = 2 * p + h
            col = slice(h * LANES, (h + 1) * LANES)
            g = S72[R * q : R * q + R, :]
            psum_o[p, :, col] = g
            W96[R * q : R * q + R, :] = adamw_step(
                p_master[p, :, col], p_m[p, :, col], p_v[p, :, col], clip * g, decay_rate
            )[0]
    g = K3[z, 0:R, :]
    ksum_o[...] = g
    W96[72 : 72 + R, :] = adamw_step(k_master[...], k_m[...], k_v[...], clip * g, decay_rate)[0]
    G[c, z, y] = W96[...].astype(BF16)

    up_y, down_y = device(y=lax.rem(y + 1, NY)), device(y=lax.rem(y + NY - 1, NY))
    ahead, behind = lax.rem(y + 1, NY), lax.rem(y + NY - 1, NY)
    own = G.at[c, z, y]
    first = [links.send(own, own, up_y), links.send(own, own, down_y)]
    first[0].wait_recv()
    lo = G.at[c, z, behind, 0:48]
    second = [links.send(lo, lo, up_y)]
    first[1].wait_recv()
    hi = G.at[c, z, ahead, 48:96]
    second.append(links.send(hi, hi, down_y))

    up_z, down_z = device(z=lax.rem(z + 1, NZ)), device(z=lax.rem(z + NZ - 1, NZ))
    far = lax.rem(y + 2, NY)
    order = (y, behind, ahead, far)

    def plane_moves(zz, yy, dev):
        ref = G.at[c, zz, yy]
        return links.send(ref, ref, dev)

    up, down, twin = {}, {}, {}
    for j in range(3):
        up[1, j] = plane_moves(z, order[j], up_z)
        down[1, j] = plane_moves(z, order[j], down_z)
    second[0].wait_recv()
    second[1].wait_recv()
    up[1, 3] = plane_moves(z, order[3], up_z)
    down[1, 3] = plane_moves(z, order[3], down_z)
    own_plane = G.at[c, z]
    twin[0, 0] = links.send(own_plane, own_plane, sibling)

    def unpack(zz):
        for k in range(NY * NC):
            block = G[k % NC, zz, k // NC].astype(F32)
            W96[...] = block
            for q in range(5):
                T5[q, R * k : R * k + R, :] = W96[R * q : R * q + R, :]
        for p in range(2):
            for h in range(2):
                pw_o[p, zz, :, h * LANES : (h + 1) * LANES] = T5[2 * p + h].astype(BF16)
        FK[x, zz] = T5[4].astype(BF16)

    up_x, down_x = device(x=lax.rem(x + 1, NX)), device(x=lax.rem(x + NX - 1, NX))
    cut_x = (slice(0, 80), slice(80, 144))
    x_first = {}

    def x_block(j):
        return lax.rem(z + (1 - 2 * c) * j - c + NZ, NZ)

    def x_start(j):
        ref = FK.at[x, x_block(j)]
        x_first[j] = (links.send(ref, ref, up_x), links.send(ref, ref, down_x))

    for d in range(1, 5):
        below, above = lax.rem(z - d + NZ, NZ), lax.rem(z + d, NZ)
        if d < 4:
            for j in range(4):
                up[d, j].wait_recv()
                if d < 3:
                    up[d + 1, j] = plane_moves(below, order[j], up_z)
                elif j < 2:
                    up[4, j] = plane_moves(below, order[j], up_z)
                down[d, j].wait_recv()
                if d < 3:
                    down[d + 1, j] = plane_moves(above, order[j], down_z)
                elif j >= 2:
                    down[4, j] = plane_moves(above, order[j], down_z)
            for way, zz in ((0, below), (1, above)):
                ref = G.at[c, zz]
                twin[d, way] = links.send(ref, ref, sibling)
        else:
            for copy in (up[4, 0], up[4, 1], down[4, 2], down[4, 3]):
                copy.wait_recv()
            ref = G.at[c, above]
            twin[4, 0] = links.send(ref, ref, sibling)
        if d == 1:
            twin[0, 0].wait_recv()
            unpack(z)
        else:
            for way, zz in ((0, lax.rem(z - d + 1 + NZ, NZ)), (1, lax.rem(z + d - 1, NZ))):
                twin[d - 1, way].wait_recv()
                unpack(zz)
            x_start(d - 2)
    twin[4, 0].wait_recv()
    unpack(lax.rem(z + 4, NZ))
    x_start(3)

    x_behind, x_ahead, x_far = lax.rem(x + NX - 1, NX), lax.rem(x + 1, NX), lax.rem(x + 2, NX)
    x_second, x_twin = {}, []
    for j in range(4):
        zz = x_block(j)
        x_first[j][0].wait_recv()
        ref = FK.at[x_behind, zz, cut_x[0]]
        lo_send = links.send(ref, ref, up_x)
        ref = FK.at[x_behind, zz]
        x_twin.append(links.send(ref, ref, sibling))
        x_first[j][1].wait_recv()
        ref = FK.at[x_ahead, zz, cut_x[1]]
        hi_send = links.send(ref, ref, down_x)
        ref = FK.at[x_ahead, zz]
        x_twin.append(links.send(ref, ref, sibling))
        x_second[j] = (lo_send, hi_send)
    for j in range(4):
        zz = x_block(j)
        for copy in x_second[j]:
            copy.wait_recv()
        ref = FK.at[x_far, zz]
        x_twin.append(links.send(ref, ref, sibling))
    for copy in x_twin:
        copy.wait_recv()

    @pl.loop(0, NZ)
    def _(zz):
        for xx in range(NX):
            kw_o[zz, :, xx * LANES : (xx + 1) * LANES] = FK[xx, zz]

    assert len(links.started) <= N_COPIES
    links.finish()


def moments_kernel(
    psum, ksum, tile, p_master, p_m, p_v, k_master, k_m, k_v, gains, g_m, g_v,
    p_new, p_m_new, p_v_new, k_new, k_m_new, k_v_new, gains_new, g_m_new, g_v_new,
):
    clip = clip_of(tile[...])
    for p in range(2):
        p_new[p], p_m_new[p], p_v_new[p] = adamw_step(p_master[p], p_m[p], p_v[p], clip * psum[p], decay_rate)
    k_new[...], k_m_new[...], k_v_new[...] = adamw_step(k_master[...], k_m[...], k_v[...], clip * ksum[...], decay_rate)
    for i in range(2):
        for h in range(2):
            col = slice(h * LANES, (h + 1) * LANES)
            row = slice(i, i + 1)
            g = tile[2 * i + h : 2 * i + h + 1, :]
            gains_new[row, col], g_m_new[row, col], g_v_new[row, col] = adamw_step(
                gains[row, col], g_m[row, col], g_v[row, col], clip * g, 0.0
            )


def shards(
    proj_grads,
    kv_grads,
    gain_grads,
    proj_master,
    proj_m,
    proj_v,
    kv_master,
    kv_m,
    kv_v,
    gains,
    gains_m,
    gains_v,
):
    vmem, anywhere = pl.BlockSpec(memory_space=pltpu.VMEM), pl.BlockSpec(memory_space=pl.ANY)
    shape = jax.ShapeDtypeStruct
    scratch = [
        ((2, 2, 1152, 256), BF16), ((2, 1152, 512), BF16),
        ((NC, NY, NZ, 40, LANES), F32), ((NC, NZ, NY, 32, LANES), F32), ((NC, NX, NY, 2, 72, LANES), F32),
        ((NY, NZ, 40, LANES), F32), ((NZ, NY, 32, LANES), F32), ((NX, NY, 2, 72, LANES), F32),
        ((ZR, LANES), F32),
        ((2, 2, 2, 4, 40, LANES), F32), ((2, 2, 4, 2, 32, LANES), F32), ((2, 2, 2, 2, 2, 72, LANES), F32),
        ((2, 4, 24, LANES), F32), ((2, 4, 16, LANES), F32), ((2, 2, 2, 16, LANES), F32), ((2, 2, 2, 72, LANES), F32),
        ((NZ, 24, LANES), F32), ((2, 4, 16, LANES), F32), ((2, 4, 8, LANES), F32),
        ((NC, 8, LANES), F32), ((NX, 8, LANES), F32), ((NY, 8, LANES), F32), ((NZ, 8, LANES), F32),
        ((72, LANES), F32), ((96, LANES), F32),
        ((NC, NZ, NY, 96, LANES), BF16), ((NX, NZ, ZR, LANES), BF16), ((5, ZR, LANES), F32),
    ]
    psum, ksum, tile, proj_weights, kv_weights = pl.pallas_call(
        step_kernel,
        name="reduce_update_gather",
        out_shape=[
            shape((2, R, 256), F32),
            shape((R, LANES), F32),
            shape((8, LANES), F32),
            shape((2, NZ, ZR, 256), BF16),
            shape((NZ, ZR, 512), BF16),
        ],
        in_specs=[anywhere, anywhere] + [vmem] * 7,
        out_specs=[vmem] * 5,
        scratch_shapes=[pltpu.VMEM(s, d) for s, d in scratch]
        + [pltpu.SemaphoreType.DMA((N_COPIES,)), pltpu.SemaphoreType.DMA((N_COPIES,)), pltpu.SemaphoreType.DMA((2,))],
        compiler_params=pltpu.CompilerParams(
            collective_id=0, has_side_effects=True, vmem_limit_bytes=56 * 1024 * 1024
        ),
    )(proj_grads, kv_grads, gain_grads, proj_master, proj_m, proj_v, kv_master, kv_m, kv_v)
    state = (proj_master, proj_m, proj_v, kv_master, kv_m, kv_v, gains, gains_m, gains_v)
    new = pl.pallas_call(
        moments_kernel,
        name="moments",
        out_shape=[shape(a.shape, F32) for a in state],
        in_specs=[vmem] * 12,
        out_specs=[vmem] * 9,
    )(psum, ksum, tile, *state)
    return (
        *new[0:3],
        proj_weights.reshape(2, 1152, 256),
        *new[3:6],
        kv_weights.reshape(1152, 512),
        *new[6:9],
    )


def solution(mesh):
    placed = (
        P("shard", None, None, "tensor"),
        P(("tensor", "shard"), None, None),
        P(("tensor", "shard"), None, None),
        P(None, "shard", "tensor"),
        P(None, "shard", "tensor"),
        P(None, "shard", "tensor"),
        P("shard", "tensor"),
        P("shard", "tensor"),
        P("shard", "tensor"),
        P(),
        P(),
        P(),
    )
    return jax.shard_map(
        shards,
        mesh=mesh,
        in_specs=placed,
        out_specs=(
            P(None, "shard", "tensor"),
            P(None, "shard", "tensor"),
            P(None, "shard", "tensor"),
            P(None, None, "tensor"),
            P("shard", "tensor"),
            P("shard", "tensor"),
            P("shard", "tensor"),
            P(),
            P(),
            P(),
            P(),
        ),
        check_vma=False,
    )
```

time: 488 us -> 116 us (0.24)
  waiting for transfers between devices: 357 us -> 0 us
  Pallas kernels: 0 us -> 103 us
  blocking collectives: 86.6 us -> 0 us
  between operations: 17.2 us -> 0.66 us
  other arithmetic: 11.1 us -> 0 us
    unnamed x5 -> x0, waiting for transfers between devices: 198 us -> none
    all_gather x2 -> x0, waiting for transfers between devices: 138 us -> none  [the longest x1 74.9 us: shards(): lax.all_gather(kv_wide, 'shard', axis=0, tiled=True)]
    pallas_call x0 -> x2, Pallas kernels: none -> 103 us  [the longest x1 101 us: shards(): pl.pallas_call(step_kernel, name='reduce_update_gather', out_shape=[shape...]
    psum x1 -> x0, blocking collectives: 78.1 us -> none  [shards(): lax.psum(owned_square, ('tensor', 'shard')) + jnp.sum(gain_sum * gain_sum)]
    reduce_scatter x1 -> x0, waiting for transfers between devices: 21.1 us -> none  [shards(): lax.psum_scatter(kv_row_part, 'tensor', scatter_dimension=1, tiled=True)]
    all_gather x1 -> x0, blocking collectives: 8.46 us -> none  [shards(): kv_wide = lax.all_gather(kv_half, 'tensor', axis=1, tiled=True)]
    reduce_sum x1 -> x0, local copies, waits for them, and re-layouts: 7.64 us -> none  [shards(): proj_local = jnp.sum(proj_grads, axis=0, dtype=jnp.float32)]
    reduce_sum x6 -> x0, other arithmetic: 7.64 us -> none  [the longest x1 2.3 us: shards(): proj_local = jnp.sum(proj_grads, axis=0, dtype=jnp.float32)]
  transfers between devices with their start and end apart: 4 -> 0, of which waited for: 4 -> 0; matrix products, arithmetic and copies ran while one was open for 1% -> 0% of each run, Pallas kernels for 0% -> 0%
where the time goes in v1:
time: 116 us; the launch traced here: 115 us
  Pallas kernels  103 us (89%)
  local copies, waits for them, and re-layouts  11.9 us (10%)
    pallas_call x1, Pallas kernels, shards(): pl.pallas_call(step_kernel, name='reduce_update_gather', out_shape=[shape...  101 us
    unnamed x10, local copies, waits for them, and re-layouts  11.9 us

profile of v1, /device:TPU:1, one launch (start us, length us, event | category | flops | bytes accessed | tf_op | source)
XLA Modules:
  0.0 115.4 jit_solution(16007976017520312855)
XLA Ops:
  0.6 1.4 %copy.23.p_master = f32[2,18,256]{2,1,0:T(8,128)} copy(f32[2,18,256]{2,0,1:T(2,128)} %param.15) | data formatting | bytes 73728 | tf_op args[3]
  2.0 1.4 %copy.24.p_m = f32[2,18,256]{2,1,0:T(8,128)} copy(f32[2,18,256]{2,0,1:T(2,128)} %param.16) | data formatting | bytes 73728 | tf_op args[4]
  3.4 1.4 %copy.25.p_v = f32[2,18,256]{2,1,0:T(8,128)} copy(f32[2,18,256]{2,0,1:T(2,128)} %param.17) | data formatting | bytes 73728 | tf_op args[5]
  4.8 101.1 %reduce_update_gather.1 = (f32[2,18,256]{2,1,0:T(8,128)}, f32[18,128]{1,0:T(8,128)}, f32[8,128]{1,0:T(8,128)}, bf16[2,8,144,256]{3,2,1,0:T(8,128)(2,1)}, bf16[8,144,512]{2,1,0:T(8,128)(2,1)}) custom-call(bf16[2,2,1152,256]{3,2,1,0:T(8,128)(2,1)} %pg.1, bf16[2,1152,512]{2,1,0:T(8,128)(2,1)} %kg.1, bf16[2,2,256]{2,1,0:T(2,128)(2,1)} %gg.1, ...), custom_call_target="tpu_custom_call" | custom-call | tf_op jit(solution)/shard_map/reduce_update_gather/pallas_call | solution.py:469
  105.9 1.8 %moments.1 = (f32[2,18,256]{2,1,0:T(8,128)}, f32[2,18,256]{2,1,0:T(8,128)}, f32[2,18,256]{2,1,0:T(8,128)}, f32[18,128]{1,0:T(8,128)}, f32[18,128]{1,0:T(8,128)},...) custom-call(f32[2,18,256]{2,1,0:T(8,128)} %get-tuple-element.25.psum, ...), custom_call_target="tpu_custom_call" | custom-call | tf_op jit(solution)/shard_map/moments/pallas_call | solution.py:488
  107.6 1.4 %copy.29 = f32[2,18,256]{2,0,1:T(2,128)} copy(f32[2,18,256]{2,1,0:T(8,128)} %get-tuple-element.39) | data formatting | bytes 73728
  109.1 1.4 %copy.30 = f32[2,18,256]{2,0,1:T(2,128)} copy(f32[2,18,256]{2,1,0:T(8,128)} %get-tuple-element.40) | data formatting | bytes 73728
  110.5 1.4 %copy.31 = f32[2,18,256]{2,0,1:T(2,128)} copy(f32[2,18,256]{2,1,0:T(8,128)} %get-tuple-element.41) | data formatting | bytes 73728
  111.9 0.0 copy-start
  111.9 2.5 %copy.34 = bf16[2,1152,256]{2,1,0:T(8,128)(2,1)} copy(bf16[2,1152,256]{2,1,0:T(8,128)(2,1)} %bitcast.3) | data formatting | bytes 2359296
  114.4 0.0 copy-done
  114.4 1.0 copy.35
Async XLA Ops:
  111.9 2.5 %copy-start = (bf16[8,144,512]{2,1,0:T(8,128)(2,1)S(1)}, bf16[8,144,512]{2,1,0:T(8,128)(2,1)}, u32[]{:S(2)}) copy-start(bf16[8,144,512]{2,1,0:T(8,128)(2,1)} %get-tuple-element.35) | copy-start | bytes 3538948

commit v2 on v1

--- a/solution.py
+++ b/solution.py
@@ -112,17 +112,25 @@
                 take(way, part, 1)
 
 
-def run(*generators):
-    waiting = list(generators)
-    while waiting:
-        waiting = [g for g in waiting if next(g, "end") != "end"]
+def scatter_direct(links, n, pos, device, view, slots):
+    copies = {}
+    for d in sorted(range(1, n), key=lambda d: -min(d, n - d)):
+        dest = lax.rem(pos + d, n)
+        copies[d] = links.send(view(dest), slots.at[d - 1], device(dest))
+    yield
+    own = view(pos)
+    total = own[...]
+    for d in sorted(range(1, n), key=lambda d: min(d, n - d)):
+        copies[d].wait_recv()
+        total = total + slots[d - 1]
+    own[...] = total
 
 
 def step_kernel(
     pg, kg, gg, p_master, p_m, p_v, k_master, k_m, k_v,
     psum_o, ksum_o, tile_o, pw_o, kw_o,
     pgv, kgv, PA, PB, KK, RA, RB, RK, T,
-    rAy, rBz, rKx, rAz0, rAz1, rBy, rKy, K3, rKz0, rKz1,
+    rAy, rBz, rKx, rAz, rBy, rKy, K3, rKz,
     tc, tx, ty, tz, S72, W96, G, FK, T5,
     send_sems, recv_sems, local_sems,
 ):
@@ -200,67 +208,53 @@
     for xx, copy in k_cores:
         copy.wait_recv()
         KK[c, xx] = KK[c, xx] + RK[xx]
-    ring_kx = scatter_ring(
-        links, NX, x, lambda i: device(x=i),
-        lambda i, part: KK.at[c, i, 2 * part : 2 * part + 2],
-        lambda way, part, d: rKx.at[(1 - way) // 2, part, d - 1],
-    )
-    next(ring_kx)
+
+    def chain_k():
+        yield from scatter_ring(
+            links, NX, x, lambda i: device(x=i),
+            lambda i, part: KK.at[c, i, 2 * part : 2 * part + 2],
+            lambda way, part, d: rKx.at[(1 - way) // 2, part, d - 1],
+        )
+        yield from scatter_direct(links, NY, y, lambda i: device(y=i), lambda i: KK.at[c, x, i], rKy)
+        K3[...] = jnp.zeros_like(K3)
+        for zz in range(NZ):
+            K3[zz, 0:R, :] = KK[c, x, y, zz // 4, R * (zz % 4) : R * (zz % 4) + R, :]
+        yield from scatter_direct(links, NZ, z, lambda i: device(z=i), lambda i: K3.at[i], rKz)
+
+    def chain_b():
+        yield from scatter_ring(
+            links, NZ, z, lambda i: device(z=i),
+            lambda i, part: PB.at[c, i, 2 * part : 2 * part + 2],
+            lambda way, part, d: rBz.at[(1 - way) // 2, part, d - 1],
+        )
+        yield from scatter_direct(links, NY, y, lambda i: device(y=i), lambda i: PB.at[c, z, i], rBy)
+
+    def chain_a():
+        yield from scatter_ring(
+            links, NY, y, lambda i: device(y=i),
+            lambda i, part: PA.at[c, i, 4 * part : 4 * part + 4],
+            lambda way, part, d: rAy.at[(1 - way) // 2, part, d - 1],
+        )
+        yield from scatter_direct(links, NZ, z, lambda i: device(z=i), lambda i: PA.at[c, y, i], rAz)
+
+    for_k, for_b, for_a = chain_k(), chain_b(), chain_a()
+    next(for_k)
     b_core.wait_recv()
 
     @pl.loop(0, NZ)
     def _(zz):
         PB[c, zz] = PB[c, zz] + RB[zz]
 
-    ring_bz = scatter_ring(
-        links, NZ, z, lambda i: device(z=i),
-        lambda i, part: PB.at[c, i, 2 * part : 2 * part + 2],
-        lambda way, part, d: rBz.at[(1 - way) // 2, part, d - 1],
-    )
-    next(ring_bz)
+    next(for_b)
     a_core.wait_recv()
 
     @pl.loop(0, NY)
     def _(yy):
         PA[c, yy] = PA[c, yy] + RA[yy]
 
-    ring_ay = scatter_ring(
-        links, NY, y, lambda i: device(y=i),
-        lambda i, part: PA.at[c, i, 4 * part : 4 * part + 4],
-        lambda way, part, d: rAy.at[(1 - way) // 2, part, d - 1],
-    )
-    next(ring_ay)
-
-    run(ring_ay, ring_bz, ring_kx)
-
-    cut_a, cut_b = (slice(0, 24), slice(24, 40)), (slice(0, 16), slice(16, 32))
-    ring_az = scatter_ring(
-        links, NZ, z, lambda i: device(z=i),
-        lambda i, part: PA.at[c, y, i, cut_a[part]],
-        lambda way, part, d: (rAz0, rAz1)[part].at[(1 - way) // 2, d - 1],
-    )
-    ring_by = scatter_ring(
-        links, NY, y, lambda i: device(y=i),
-        lambda i, part: PB.at[c, z, i, cut_b[part]],
-        lambda way, part, d: rBy.at[(1 - way) // 2, part, d - 1],
-    )
-    ring_ky = scatter_ring(
-        links, NY, y, lambda i: device(y=i),
-        lambda i, part: KK.at[c, x, i, part],
-        lambda way, part, d: rKy.at[(1 - way) // 2, part, d - 1],
-    )
-    run(ring_ky, ring_az, ring_by)
-
-    K3[...] = jnp.zeros_like(K3)
-    for zz in range(NZ):
-        K3[zz, 0:R, :] = KK[c, x, y, zz // 4, R * (zz % 4) : R * (zz % 4) + R, :]
-    cut_k = (slice(0, 16), slice(16, 24))
-    ring_kz = scatter_ring(
-        links, NZ, z, lambda i: device(z=i),
-        lambda i, part: K3.at[i, cut_k[part]],
-        lambda way, part, d: (rKz0, rKz1)[part].at[(1 - way) // 2, d - 1],
-    )
-    run(ring_kz)
+    next(for_a)
+    for chain in (for_b, for_b, for_a, for_k, for_b, for_b, for_a, for_k, for_b, for_a, for_k, for_k):
+        next(chain, None)
 
     S72[0:40, :] = PA[c, y, z]
     S72[40:72, :] = PB[c, z, y]
@@ -292,9 +286,9 @@
             q = 2 * p + h
             col = slice(h * LANES, (h + 1) * LANES)
             g = S72[R * q : R * q + R, :]
-            psum_o[p, :, col] = g
+            psum_o[:, p, col] = g
             W96[R * q : R * q + R, :] = adamw_step(
-                p_master[p, :, col], p_m[p, :, col], p_v[p, :, col], clip * g, decay_rate
+                p_master[:, p, col], p_m[:, p, col], p_v[:, p, col], clip * g, decay_rate
             )[0]
     g = K3[z, 0:R, :]
     ksum_o[...] = g
@@ -421,12 +415,28 @@
 
 
 def moments_kernel(
-    psum, ksum, tile, p_master, p_m, p_v, k_master, k_m, k_v, gains, g_m, g_v,
-    p_new, p_m_new, p_v_new, k_new, k_m_new, k_v_new, gains_new, g_m_new, g_v_new,
+    psum, ksum, tile, pw, kw, p_master, p_m, p_v, k_master, k_m, k_v, gains, g_m, g_v,
+    p_new, p_m_new, p_v_new, k_new, k_m_new, k_v_new, gains_new, g_m_new, g_v_new, pw_new, kw_new,
+    pwv, kwv, in_sems, out_sems,
 ):
+    pieces = []
+    for i in range(4):
+        p, half = i // 2, pl.ds(4 * (i % 2), 4)
+        pieces.append((pw.at[p, half], pwv.at[p, half], pw_new.at[p, half]))
+        pair = pl.ds(2 * i, 2)
+        pieces.append((kw.at[pair], kwv.at[pair], kw_new.at[pair]))
+    into = [pltpu.make_async_copy(src, mid, in_sems.at[i]) for i, (src, mid, _) in enumerate(pieces)]
+    out = [pltpu.make_async_copy(mid, dst, out_sems.at[i]) for i, (_, mid, dst) in enumerate(pieces)]
+    for copy in into:
+        copy.start()
+    for arrive, leave in zip(into, out):
+        arrive.wait()
+        leave.start()
     clip = clip_of(tile[...])
-    for p in range(2):
-        p_new[p], p_m_new[p], p_v_new[p] = adamw_step(p_master[p], p_m[p], p_v[p], clip * psum[p], decay_rate)
+    scale = jnp.reshape(clip, (1, 1, 1))
+    p_new[...], p_m_new[...], p_v_new[...] = adamw_step(
+        p_master[...], p_m[...], p_v[...], scale * psum[...], decay_rate
+    )
     k_new[...], k_m_new[...], k_v_new[...] = adamw_step(k_master[...], k_m[...], k_v[...], clip * ksum[...], decay_rate)
     for i in range(2):
         for h in range(2):
@@ -436,6 +446,8 @@
             gains_new[row, col], g_m_new[row, col], g_v_new[row, col] = adamw_step(
                 gains[row, col], g_m[row, col], g_v[row, col], clip * g, 0.0
             )
+    for leave in out:
+        leave.wait()
 
 
 def shards(
@@ -452,6 +464,7 @@
     gains_m,
     gains_v,
 ):
+    proj_master, proj_m, proj_v = (jnp.transpose(a, (1, 0, 2)) for a in (proj_master, proj_m, proj_v))
     vmem, anywhere = pl.BlockSpec(memory_space=pltpu.VMEM), pl.BlockSpec(memory_space=pl.ANY)
     shape = jax.ShapeDtypeStruct
     scratch = [
@@ -460,8 +473,8 @@
         ((NY, NZ, 40, LANES), F32), ((NZ, NY, 32, LANES), F32), ((NX, NY, 2, 72, LANES), F32),
         ((ZR, LANES), F32),
         ((2, 2, 2, 4, 40, LANES), F32), ((2, 2, 4, 2, 32, LANES), F32), ((2, 2, 2, 2, 2, 72, LANES), F32),
-        ((2, 4, 24, LANES), F32), ((2, 4, 16, LANES), F32), ((2, 2, 2, 16, LANES), F32), ((2, 2, 2, 72, LANES), F32),
-        ((NZ, 24, LANES), F32), ((2, 4, 16, LANES), F32), ((2, 4, 8, LANES), F32),
+        ((NZ - 1, 40, LANES), F32), ((NY - 1, 32, LANES), F32), ((NY - 1, 2, 72, LANES), F32),
+        ((NZ, 24, LANES), F32), ((NZ - 1, 24, LANES), F32),
         ((NC, 8, LANES), F32), ((NX, 8, LANES), F32), ((NY, 8, LANES), F32), ((NZ, 8, LANES), F32),
         ((72, LANES), F32), ((96, LANES), F32),
         ((NC, NZ, NY, 96, LANES), BF16), ((NX, NZ, ZR, LANES), BF16), ((5, ZR, LANES), F32),
@@ -470,7 +483,7 @@
         step_kernel,
         name="reduce_update_gather",
         out_shape=[
-            shape((2, R, 256), F32),
+            shape((R, 2, 256), F32),
             shape((R, LANES), F32),
             shape((8, LANES), F32),
             shape((2, NZ, ZR, 256), BF16),
@@ -488,15 +501,21 @@
     new = pl.pallas_call(
         moments_kernel,
         name="moments",
-        out_shape=[shape(a.shape, F32) for a in state],
-        in_specs=[vmem] * 12,
-        out_specs=[vmem] * 9,
-    )(psum, ksum, tile, *state)
+        out_shape=[shape(a.shape, F32) for a in state] + [shape(a.shape, BF16) for a in (proj_weights, kv_weights)],
+        in_specs=[vmem] * 3 + [anywhere] * 2 + [vmem] * 9,
+        out_specs=[vmem] * 9 + [anywhere] * 2,
+        scratch_shapes=[
+            pltpu.VMEM(proj_weights.shape, BF16),
+            pltpu.VMEM(kv_weights.shape, BF16),
+            pltpu.SemaphoreType.DMA((8,)),
+            pltpu.SemaphoreType.DMA((8,)),
+        ],
+    )(psum, ksum, tile, proj_weights, kv_weights, *state)
     return (
-        *new[0:3],
-        proj_weights.reshape(2, 1152, 256),
+        *(jnp.transpose(a, (1, 0, 2)) for a in new[0:3]),
+        new[9].reshape(2, 1152, 256),
         *new[3:6],
-        kv_weights.reshape(1152, 512),
+        new[10].reshape(1152, 512),
         *new[6:9],
     )
 

time: 116 us -> 86.3 us (0.74)
  Pallas kernels: 103 us -> 85.4 us
  local copies, waits for them, and re-layouts: 11.9 us -> 0 us
    pallas_call x1, Pallas kernels: 101 us -> 81.4 us  [shards(): pl.pallas_call(step_kernel, name='reduce_update_gather', out_shape=[shape...]
    unnamed x10 -> x0, local copies, waits for them, and re-layouts: 11.9 us -> none
    pallas_call x1, Pallas kernels: 1.75 us -> 4.07 us  [shards(): pl.pallas_call(moments_kernel, name='moments', out_shape=[shape(a.shape,...]
where the time goes in v2:
time: 86.3 us; the launch traced here: 86.1 us
  Pallas kernels  85.4 us (99%)
    pallas_call x1, Pallas kernels, shards(): pl.pallas_call(step_kernel, name='reduce_update_gather', out_shape=[shape...  81.4 us
    pallas_call x1, Pallas kernels, shards(): pl.pallas_call(moments_kernel, name='moments', out_shape=[shape(a.shape,...  4.07 us

profile of v2, /device:TPU:1, one launch (start us, length us, event | category | flops | bytes accessed | tf_op | source)
XLA Modules:
  0.0 86.1 jit_solution(17898562322648941888)
XLA Ops:
  0.6 81.4 %reduce_update_gather.1 = (f32[18,2,256]{2,1,0:T(2,128)}, f32[18,128]{1,0:T(8,128)}, f32[8,128]{1,0:T(8,128)}, bf16[2,8,144,256]{3,2,1,0:T(8,128)(2,1)}, bf16[8,144,512]{2,1,0:T(8,128)(2,1)}) custom-call(bf16[2,2,1152,256]{3,2,1,0:T(8,128)(2,1)} %pg.1, bf16[2,1152,512]{2,1,0:T(8,128)(2,1)} %kg.1, bf16[2,2,256]{2,1,0:T(2,128)(2,1)} %gg.1, ...), custom_call_target="tpu_custom_call" | custom-call | tf_op jit(solution)/shard_map/reduce_update_gather/pallas_call | solution.py:482
  82.0 4.1 %moments.1 = (f32[18,2,256]{2,1,0:T(2,128)}, f32[18,2,256]{2,1,0:T(2,128)}, f32[18,2,256]{2,1,0:T(2,128)}, f32[18,128]{1,0:T(8,128)}, f32[18,128]{1,0:T(8,128)},...) custom-call(f32[18,2,256]{2,1,0:T(2,128)} %get-tuple-element.27.psum, ...), custom_call_target="tpu_custom_call" | custom-call | tf_op jit(solution)/shard_map/moments/pallas_call | solution.py:501

commit v3 on v2

--- a/solution.py
+++ b/solution.py
@@ -182,8 +182,37 @@
             barrier_done = True
         k_cores.append((xx, links.send(KK.at[oc, xx], RK.at[xx], sibling)))
 
+    def chain_k():
+        yield from scatter_ring(
+            links, NX, x, lambda i: device(x=i),
+            lambda i, part: KK.at[c, i, 2 * part : 2 * part + 2],
+            lambda way, part, d: rKx.at[(1 - way) // 2, part, d - 1],
+        )
+        yield from scatter_direct(links, NY, y, lambda i: device(y=i), lambda i: KK.at[c, x, i], rKy)
+        K3[...] = jnp.zeros_like(K3)
+        for zz in range(NZ):
+            K3[zz, 0:R, :] = KK[c, x, y, zz // 4, R * (zz % 4) : R * (zz % 4) + R, :]
+        yield from scatter_direct(links, NZ, z, lambda i: device(z=i), lambda i: K3.at[i], rKz)
+
+    def chain_b():
+        yield from scatter_ring(
+            links, NZ, z, lambda i: device(z=i),
+            lambda i, part: PB.at[c, i, 2 * part : 2 * part + 2],
+            lambda way, part, d: rBz.at[(1 - way) // 2, part, d - 1],
+        )
+        yield from scatter_direct(links, NY, y, lambda i: device(y=i), lambda i: PB.at[c, z, i], rBy)
+
+    def chain_a():
+        yield from scatter_ring(
+            links, NY, y, lambda i: device(y=i),
+            lambda i, part: PA.at[c, i, 4 * part : 4 * part + 4],
+            lambda way, part, d: rAy.at[(1 - way) // 2, part, d - 1],
+        )
+        yield from scatter_direct(links, NZ, z, lambda i: device(z=i), lambda i: PA.at[c, y, i], rAz)
+
+    for_k, for_b, for_a = chain_k(), chain_b(), chain_a()
     p_in.wait()
-    for p in range(2):
+    for p in (1, 0):
 
         @pl.loop(0, NZ)
         def _(zz):
@@ -202,43 +231,15 @@
                     else:
                         PB[cc, zz, yy, 14:32, :] = T[R * k : R * k + R, :]
 
-    b_core = links.send(PB.at[oc], RB, sibling)
+        if p == 1:
+            b_core = links.send(PB.at[oc], RB, sibling)
+            for xx, copy in k_cores:
+                copy.wait_recv()
+                KK[c, xx] = KK[c, xx] + RK[xx]
+            next(for_k)
+
     a_core = links.send(PA.at[oc], RA, sibling)
 
-    for xx, copy in k_cores:
-        copy.wait_recv()
-        KK[c, xx] = KK[c, xx] + RK[xx]
-
-    def chain_k():
-        yield from scatter_ring(
-            links, NX, x, lambda i: device(x=i),
-            lambda i, part: KK.at[c, i, 2 * part : 2 * part + 2],
-            lambda way, part, d: rKx.at[(1 - way) // 2, part, d - 1],
-        )
-        yield from scatter_direct(links, NY, y, lambda i: device(y=i), lambda i: KK.at[c, x, i], rKy)
-        K3[...] = jnp.zeros_like(K3)
-        for zz in range(NZ):
-            K3[zz, 0:R, :] = KK[c, x, y, zz // 4, R * (zz % 4) : R * (zz % 4) + R, :]
-        yield from scatter_direct(links, NZ, z, lambda i: device(z=i), lambda i: K3.at[i], rKz)
-
-    def chain_b():
-        yield from scatter_ring(
-            links, NZ, z, lambda i: device(z=i),
-            lambda i, part: PB.at[c, i, 2 * part : 2 * part + 2],
-            lambda way, part, d: rBz.at[(1 - way) // 2, part, d - 1],
-        )
-        yield from scatter_direct(links, NY, y, lambda i: device(y=i), lambda i: PB.at[c, z, i], rBy)
-
-    def chain_a():
-        yield from scatter_ring(
-            links, NY, y, lambda i: device(y=i),
-            lambda i, part: PA.at[c, i, 4 * part : 4 * part + 4],
-            lambda way, part, d: rAy.at[(1 - way) // 2, part, d - 1],
-        )
-        yield from scatter_direct(links, NZ, z, lambda i: device(z=i), lambda i: PA.at[c, y, i], rAz)
-
-    for_k, for_b, for_a = chain_k(), chain_b(), chain_a()
-    next(for_k)
     b_core.wait_recv()
 
     @pl.loop(0, NZ)
@@ -246,6 +247,7 @@
         PB[c, zz] = PB[c, zz] + RB[zz]
 
     next(for_b)
+    next(for_k)
     a_core.wait_recv()
 
     @pl.loop(0, NY)
@@ -253,7 +255,7 @@
         PA[c, yy] = PA[c, yy] + RA[yy]
 
     next(for_a)
-    for chain in (for_b, for_b, for_a, for_k, for_b, for_b, for_a, for_k, for_b, for_a, for_k, for_k):
+    for chain in (for_b, for_k, for_b, for_a, for_b, for_a, for_k, for_b, for_a, for_b, for_k):
         next(chain, None)
 
     S72[0:40, :] = PA[c, y, z]
@@ -297,17 +299,11 @@
 
     up_y, down_y = device(y=lax.rem(y + 1, NY)), device(y=lax.rem(y + NY - 1, NY))
     ahead, behind = lax.rem(y + 1, NY), lax.rem(y + NY - 1, NY)
+    far = lax.rem(y + 2, NY)
     own = G.at[c, z, y]
-    first = [links.send(own, own, up_y), links.send(own, own, down_y)]
-    first[0].wait_recv()
-    lo = G.at[c, z, behind, 0:48]
-    second = [links.send(lo, lo, up_y)]
-    first[1].wait_recv()
-    hi = G.at[c, z, ahead, 48:96]
-    second.append(links.send(hi, hi, down_y))
+    y_copies = [links.send(own, own, device(y=far)), links.send(own, own, up_y), links.send(own, own, down_y)]
 
     up_z, down_z = device(z=lax.rem(z + 1, NZ)), device(z=lax.rem(z + NZ - 1, NZ))
-    far = lax.rem(y + 2, NY)
     order = (y, behind, ahead, far)
 
     def plane_moves(zz, yy, dev):
@@ -315,13 +311,11 @@
         return links.send(ref, ref, dev)
 
     up, down, twin = {}, {}, {}
-    for j in range(3):
+    for j, copy in enumerate((None, y_copies[1], y_copies[2], y_copies[0])):
+        if copy is not None:
+            copy.wait_recv()
         up[1, j] = plane_moves(z, order[j], up_z)
         down[1, j] = plane_moves(z, order[j], down_z)
-    second[0].wait_recv()
-    second[1].wait_recv()
-    up[1, 3] = plane_moves(z, order[3], up_z)
-    down[1, 3] = plane_moves(z, order[3], down_z)
     own_plane = G.at[c, z]
     twin[0, 0] = links.send(own_plane, own_plane, sibling)
 
@@ -337,7 +331,7 @@
         FK[x, zz] = T5[4].astype(BF16)
 
     up_x, down_x = device(x=lax.rem(x + 1, NX)), device(x=lax.rem(x + NX - 1, NX))
-    cut_x = (slice(0, 80), slice(80, 144))
+    over_x = device(x=lax.rem(x + 2, NX))
     x_first = {}
 
     def x_block(j):
@@ -345,7 +339,7 @@
 
     def x_start(j):
         ref = FK.at[x, x_block(j)]
-        x_first[j] = (links.send(ref, ref, up_x), links.send(ref, ref, down_x))
+        x_first[j] = tuple(links.send(ref, ref, to) for to in (over_x, up_x, down_x))
 
     for d in range(1, 5):
         below, above = lax.rem(z - d + NZ, NZ), lax.rem(z + d, NZ)
@@ -382,26 +376,13 @@
     x_start(3)
 
     x_behind, x_ahead, x_far = lax.rem(x + NX - 1, NX), lax.rem(x + 1, NX), lax.rem(x + 2, NX)
-    x_second, x_twin = {}, []
+    x_twin = []
     for j in range(4):
         zz = x_block(j)
-        x_first[j][0].wait_recv()
-        ref = FK.at[x_behind, zz, cut_x[0]]
-        lo_send = links.send(ref, ref, up_x)
-        ref = FK.at[x_behind, zz]
-        x_twin.append(links.send(ref, ref, sibling))
-        x_first[j][1].wait_recv()
-        ref = FK.at[x_ahead, zz, cut_x[1]]
-        hi_send = links.send(ref, ref, down_x)
-        ref = FK.at[x_ahead, zz]
-        x_twin.append(links.send(ref, ref, sibling))
-        x_second[j] = (lo_send, hi_send)
-    for j in range(4):
-        zz = x_block(j)
-        for copy in x_second[j]:
-            copy.wait_recv()
-        ref = FK.at[x_far, zz]
-        x_twin.append(links.send(ref, ref, sibling))
+        for number, xx in ((1, x_behind), (2, x_ahead), (0, x_far)):
+            x_first[j][number].wait_recv()
+            ref = FK.at[xx, zz]
+            x_twin.append(links.send(ref, ref, sibling))
     for copy in x_twin:
         copy.wait_recv()
 

time: 86.3 us -> 86.9 us (level)
  no operation moved by 1% of the time
where the time goes in v3:
time: 86.9 us; the launch traced here: 86.6 us
  Pallas kernels  86 us (99%)
    pallas_call x1, Pallas kernels, shards(): pl.pallas_call(step_kernel, name='reduce_update_gather', out_shape=[shape...  81.9 us
    pallas_call x1, Pallas kernels, shards(): pl.pallas_call(moments_kernel, name='moments', out_shape=[shape(a.shape,...  4.07 us

profile of v3, /device:TPU:1, one launch (start us, length us, event | category | flops | bytes accessed | tf_op | source)
XLA Modules:
  0.0 86.6 jit_solution(13383773334880059308)
XLA Ops:
  0.6 81.9 %reduce_update_gather.1 = (f32[18,2,256]{2,1,0:T(2,128)}, f32[18,128]{1,0:T(8,128)}, f32[8,128]{1,0:T(8,128)}, bf16[2,8,144,256]{3,2,1,0:T(8,128)(2,1)}, bf16[8,144,512]{2,1,0:T(8,128)(2,1)}) custom-call(bf16[2,2,1152,256]{3,2,1,0:T(8,128)(2,1)} %pg.1, bf16[2,1152,512]{2,1,0:T(8,128)(2,1)} %kg.1, bf16[2,2,256]{2,1,0:T(2,128)(2,1)} %gg.1, ...), custom_call_target="tpu_custom_call" | custom-call | tf_op jit(solution)/shard_map/reduce_update_gather/pallas_call | solution.py:463
  82.6 4.1 %moments.1 = (f32[18,2,256]{2,1,0:T(2,128)}, f32[18,2,256]{2,1,0:T(2,128)}, f32[18,2,256]{2,1,0:T(2,128)}, f32[18,128]{1,0:T(8,128)}, f32[18,128]{1,0:T(8,128)},...) custom-call(f32[18,2,256]{2,1,0:T(2,128)} %get-tuple-element.27.psum, ...), custom_call_target="tpu_custom_call" | custom-call | tf_op jit(solution)/shard_map/moments/pallas_call | solution.py:482

commit v4 on v2

--- a/solution.py
+++ b/solution.py
@@ -131,7 +131,7 @@
     psum_o, ksum_o, tile_o, pw_o, kw_o,
     pgv, kgv, PA, PB, KK, RA, RB, RK, T,
     rAy, rBz, rKx, rAz, rBy, rKy, K3, rKz,
-    tc, tx, ty, tz, S72, W96, G, FK, T5,
+    tc, txy, tz, S72, W96, G, FK, T5,
     send_sems, recv_sems, local_sems,
 ):
     shard, x = lax.axis_index("shard"), lax.axis_index("tensor")
@@ -149,6 +149,7 @@
     others += [device(x=lax.rem(x + d, NX)) for d in range(1, NX)]
     others += [device(y=lax.rem(y + d, NY)) for d in range(1, NY)]
     others += [device(z=lax.rem(z + d, NZ)) for d in range(1, NZ)]
+    others += [device(x=lax.rem(x + i, NX), y=lax.rem(y + j, NY)) for i in range(1, NX) for j in range(1, NY)]
 
     k_in = links.local(kg, kgv)
     p_in = links.local(pg, pgv)
@@ -263,8 +264,7 @@
     tc[c, 4:5, :] = squares
     for slots, n, me, where in (
         (tc, NC, c, lambda i: device(c=i)),
-        (tx, NX, x, lambda i: device(x=i)),
-        (ty, NY, y, lambda i: device(y=i)),
+        (txy, NX * NY, x * NY + y, lambda i: device(x=lax.div(i, NY), y=lax.rem(i, NY))),
         (tz, NZ, z, lambda i: device(z=i)),
     ):
         if slots is not tc:
@@ -297,17 +297,11 @@
 
     up_y, down_y = device(y=lax.rem(y + 1, NY)), device(y=lax.rem(y + NY - 1, NY))
     ahead, behind = lax.rem(y + 1, NY), lax.rem(y + NY - 1, NY)
+    far = lax.rem(y + 2, NY)
     own = G.at[c, z, y]
-    first = [links.send(own, own, up_y), links.send(own, own, down_y)]
-    first[0].wait_recv()
-    lo = G.at[c, z, behind, 0:48]
-    second = [links.send(lo, lo, up_y)]
-    first[1].wait_recv()
-    hi = G.at[c, z, ahead, 48:96]
-    second.append(links.send(hi, hi, down_y))
+    y_copies = [links.send(own, own, device(y=far)), links.send(own, own, up_y), links.send(own, own, down_y)]
 
     up_z, down_z = device(z=lax.rem(z + 1, NZ)), device(z=lax.rem(z + NZ - 1, NZ))
-    far = lax.rem(y + 2, NY)
     order = (y, behind, ahead, far)
 
     def plane_moves(zz, yy, dev):
@@ -315,13 +309,11 @@
         return links.send(ref, ref, dev)
 
     up, down, twin = {}, {}, {}
-    for j in range(3):
+    for j, copy in enumerate((None, y_copies[1], y_copies[2], y_copies[0])):
+        if copy is not None:
+            copy.wait_recv()
         up[1, j] = plane_moves(z, order[j], up_z)
         down[1, j] = plane_moves(z, order[j], down_z)
-    second[0].wait_recv()
-    second[1].wait_recv()
-    up[1, 3] = plane_moves(z, order[3], up_z)
-    down[1, 3] = plane_moves(z, order[3], down_z)
     own_plane = G.at[c, z]
     twin[0, 0] = links.send(own_plane, own_plane, sibling)
 
@@ -337,7 +329,7 @@
         FK[x, zz] = T5[4].astype(BF16)
 
     up_x, down_x = device(x=lax.rem(x + 1, NX)), device(x=lax.rem(x + NX - 1, NX))
-    cut_x = (slice(0, 80), slice(80, 144))
+    over_x = device(x=lax.rem(x + 2, NX))
     x_first = {}
 
     def x_block(j):
@@ -345,7 +337,7 @@
 
     def x_start(j):
         ref = FK.at[x, x_block(j)]
-        x_first[j] = (links.send(ref, ref, up_x), links.send(ref, ref, down_x))
+        x_first[j] = tuple(links.send(ref, ref, to) for to in (over_x, up_x, down_x))
 
     for d in range(1, 5):
         below, above = lax.rem(z - d + NZ, NZ), lax.rem(z + d, NZ)
@@ -382,26 +374,13 @@
     x_start(3)
 
     x_behind, x_ahead, x_far = lax.rem(x + NX - 1, NX), lax.rem(x + 1, NX), lax.rem(x + 2, NX)
-    x_second, x_twin = {}, []
+    x_twin = []
     for j in range(4):
         zz = x_block(j)
-        x_first[j][0].wait_recv()
-        ref = FK.at[x_behind, zz, cut_x[0]]
-        lo_send = links.send(ref, ref, up_x)
-        ref = FK.at[x_behind, zz]
-        x_twin.append(links.send(ref, ref, sibling))
-        x_first[j][1].wait_recv()
-        ref = FK.at[x_ahead, zz, cut_x[1]]
-        hi_send = links.send(ref, ref, down_x)
-        ref = FK.at[x_ahead, zz]
-        x_twin.append(links.send(ref, ref, sibling))
-        x_second[j] = (lo_send, hi_send)
-    for j in range(4):
-        zz = x_block(j)
-        for copy in x_second[j]:
-            copy.wait_recv()
-        ref = FK.at[x_far, zz]
-        x_twin.append(links.send(ref, ref, sibling))
+        for number, xx in ((1, x_behind), (2, x_ahead), (0, x_far)):
+            x_first[j][number].wait_recv()
+            ref = FK.at[xx, zz]
+            x_twin.append(links.send(ref, ref, sibling))
     for copy in x_twin:
         copy.wait_recv()
 
@@ -475,7 +454,7 @@
         ((2, 2, 2, 4, 40, LANES), F32), ((2, 2, 4, 2, 32, LANES), F32), ((2, 2, 2, 2, 2, 72, LANES), F32),
         ((NZ - 1, 40, LANES), F32), ((NY - 1, 32, LANES), F32), ((NY - 1, 2, 72, LANES), F32),
         ((NZ, 24, LANES), F32), ((NZ - 1, 24, LANES), F32),
-        ((NC, 8, LANES), F32), ((NX, 8, LANES), F32), ((NY, 8, LANES), F32), ((NZ, 8, LANES), F32),
+        ((NC, 8, LANES), F32), ((NX * NY, 8, LANES), F32), ((NZ, 8, LANES), F32),
         ((72, LANES), F32), ((96, LANES), F32),
         ((NC, NZ, NY, 96, LANES), BF16), ((NX, NZ, ZR, LANES), BF16), ((5, ZR, LANES), F32),
     ]

time: 86.3 us -> 82.4 us (0.955)
  Pallas kernels: 85.4 us -> 81.5 us
    pallas_call x1, Pallas kernels: 81.4 us -> 77.5 us  [shards(): pl.pallas_call(step_kernel, name='reduce_update_gather', out_shape=[shape...]
where the time goes in v4:
time: 82.4 us; the launch traced here: 82.2 us
  Pallas kernels  81.5 us (99%)
    pallas_call x1, Pallas kernels, shards(): pl.pallas_call(step_kernel, name='reduce_update_gather', out_shape=[shape...  77.5 us
    pallas_call x1, Pallas kernels, shards(): pl.pallas_call(moments_kernel, name='moments', out_shape=[shape(a.shape,...  4.07 us

profile of v4, /device:TPU:1, one launch (start us, length us, event | category | flops | bytes accessed | tf_op | source)
XLA Modules:
  0.0 82.2 jit_solution(2336592066122684208)
XLA Ops:
  0.6 77.5 %reduce_update_gather.1 = (f32[18,2,256]{2,1,0:T(2,128)}, f32[18,128]{1,0:T(8,128)}, f32[8,128]{1,0:T(8,128)}, bf16[2,8,144,256]{3,2,1,0:T(8,128)(2,1)}, bf16[8,144,512]{2,1,0:T(8,128)(2,1)}) custom-call(bf16[2,2,1152,256]{3,2,1,0:T(8,128)(2,1)} %pg.1, bf16[2,1152,512]{2,1,0:T(8,128)(2,1)} %kg.1, bf16[2,2,256]{2,1,0:T(2,128)(2,1)} %gg.1, ...), custom_call_target="tpu_custom_call" | custom-call | tf_op jit(solution)/shard_map/reduce_update_gather/pallas_call | solution.py:461
  78.1 4.1 %moments.1 = (f32[18,2,256]{2,1,0:T(2,128)}, f32[18,2,256]{2,1,0:T(2,128)}, f32[18,2,256]{2,1,0:T(2,128)}, f32[18,128]{1,0:T(8,128)}, f32[18,128]{1,0:T(8,128)},...) custom-call(f32[18,2,256]{2,1,0:T(2,128)} %get-tuple-element.27.psum, ...), custom_call_target="tpu_custom_call" | custom-call | tf_op jit(solution)/shard_map/moments/pallas_call | solution.py:480
